TPU v7x, 256 devices: a whole 4x4x8 slice. The times are simulated.
256 devices in a mesh: row: 16 (over z, core), col: 16 (over x, y).
Axes of the slice: x: 4, y: 4, z: 8, core: 2. Of those that a mesh axis runs over, the one named last changes fastest.
Arguments:
- tensor: float32 [12, 8192, 8192], P(None, 'row', 'col'), may hold values from -6 to 6
- factor_b: float32 [8192, 128], P(('col', 'row')), may hold values from -0.0625 to 0.0625
- factor_c: float32 [12, 128], replicated, may hold values from -1.75 to 1.75
Outputs:
- a_update: float32 [8192, 128], P(('row', 'col'))
- b_update: float32 [8192, 128], P(('col', 'row'))
All inputs are finite; a program needn't handle non-finite values.
Results may differ from a plain program's by a relative error of at most 0.00012.
Values sent between devices are 32-bit elements; how exact they have to be, the bound alone decides.
No kernel may reach another device: no remote copies, remote signals or barrier semaphores. Data moves between devices by JAX's collectives and lax.ppermute only.
A program may use at most 64 MiB of HBM per device.

v0:
```python
import jax
import jax.numpy as jnp
from jax import lax
from jax.sharding import PartitionSpec as P

EPSILON = 1e-06


def solve_system(rhs, system):
    highest = lax.Precision.HIGHEST
    lower = jnp.linalg.cholesky(system)
    inverse = jax.scipy.linalg.cho_solve(
        (lower, True), jnp.eye(system.shape[0], dtype=system.dtype)
    )
    return jnp.dot(rhs, inverse, precision=highest)


def gram_of(matrix):
    return jnp.dot(matrix.T, matrix, precision=lax.Precision.HIGHEST)


def per_device(tensor, factor_b, factor_c):
    highest = lax.Precision.HIGHEST
    rows_block = tensor.shape[1]
    cols_block = tensor.shape[2]
    rank_width = factor_c.shape[1]
    owned_a = rows_block // lax.axis_size("col")
    owned_b = cols_block // lax.axis_size("row")
    c_gram = gram_of(factor_c)
    empty_b = jnp.zeros((cols_block, rank_width), jnp.float32)
    gram_b = lax.psum(gram_of(factor_b), ("row", "col"))
    block = tensor
    khatri = factor_c[:, None, :] * lax.all_gather(factor_b, "row", axis=0, tiled=True)[None, :, :]
    partial_a = jnp.einsum("kij,kjr->ir", block, khatri, precision=highest)
    whole_a = lax.psum(partial_a, "col")
    summed_a = lax.dynamic_slice_in_dim(whole_a, lax.axis_index("col") * owned_a, owned_a, 0)
    a_update = solve_system(summed_a, c_gram * gram_b)
    squares = lax.psum(jnp.sum(a_update * a_update, axis=0), ("row", "col"))
    factor_a = a_update / jnp.sqrt(squares + EPSILON)
    gram_a = lax.psum(gram_of(factor_a), ("row", "col"))
    block = tensor
    khatri = factor_c[:, None, :] * lax.all_gather(factor_a, "col", axis=0, tiled=True)[None, :, :]
    partial_b = empty_b + jnp.einsum("kij,kir->jr", block, khatri, precision=highest)
    whole_b = lax.psum(partial_b, "row")
    summed_b = lax.dynamic_slice_in_dim(whole_b, lax.axis_index("row") * owned_b, owned_b, 0)
    b_update = solve_system(summed_b, c_gram * gram_a)
    return (a_update, b_update)


def solution(mesh):
    placed = (P(None, "row", "col"), P(("col", "row"), None), P())
    return jax.shard_map(
        per_device,
        mesh=mesh,
        in_specs=placed,
        out_specs=(P(("row", "col"), None), P(("col", "row"), None)),
        check_vma=False,
    )
```

profile of v0, /device:TPU:1, one launch (start us, length us, event | category | flops | bytes accessed | tf_op | source)
XLA Modules:
  0.0 809.7 jit_solution(5450451104905007428)
XLA Ops:
  7.2 1.7 fusion.35
  8.9 0.0 all-reduce.5.cloned.1.call-start
  9.0 22.3 %all_gather.6 = f32[512,128]{1,0:T(8,128)S(1)} all-gather(f32[32,128]{1,0:T(8,128)} %param.7), channel_id=1, replica_groups=mesh['row'=16,'col'=16] {'row'}, dimensions={0}, use_global_device_ids=true | all-gather | bytes 278528 | tf_op jit(solution)/shard_map/all_gather | solution.py:33
  31.2 18.3 %fusion.8 = f32[512,128]{0,1:T(8,128)} fusion(f32[12,512,512]{2,1,0:T(8,128)} %param.6, f32[512,128]{1,0:T(8,128)S(1)} %all_gather.6, f32[12,128]{1,0:T(8,128)} %param.8), kind=kOutput, calls=%fused_computation.8 | convolution fusion | flops 4832624640 | bytes 13113344 | tf_op jit(solution)/shard_map/kij,kjr->ir/dot_general | solution.py:34
  49.6 0.2 all-reduce.11.cloned.1.call-start
  49.8 209.2 %all-reduce.7.cloned.1.call-done = f32[128,128]{0,1:T(8,128)} async-done(((f32[128,128]{0,1:T(8,128)}), f32[128,128]{0,1:T(8,128)}) %all-reduce.7.cloned.1.call-update) | async-done | bytes 65552 | tf_op jit(solution)/shard_map/psum | solution.py:31
  259.1 1.1 fusion.34
  260.2 0.1 copy.7
  260.3 11.7 %cholesky.44 = f32[128,128]{1,0:T(8,128)S(1)} custom-call(f32[128,128]{1,0:T(8,128)S(1)} %fusion.27), custom_call_target="Cholesky" | custom-call | tf_op jit(solution)/shard_map/jit(cholesky)/cholesky | solution.py:11
  272.1 0.6 compare_reduce_fusion.1
  272.7 0.7 fusion.18
  273.4 9.8 %custom-call.8 = f32[1,128,128]{1,2,0:T(8,128)S(1)} custom-call(f32[1,128,128]{2,1,0:T(8,128)S(1)} %fusion.18), custom_call_target="InvertDiagBlocksLowerTriangular" | custom-call | tf_op jit(solution)/shard_map/jit(_cho_solve)/triangular_solve | solution.py:12
  283.2 0.3 fusion.16
  283.5 0.2 fusion.24
  283.7 68.0 %all-reduce.5.cloned.1.call-done = f32[512,128]{0,1:T(8,128)} async-done(((f32[512,128]{0,1:T(8,128)}), f32[512,128]{0,1:T(8,128)}) %all-reduce.5.cloned.1.call-update) | async-done | bytes 262160 | tf_op jit(solution)/shard_map/psum | solution.py:35
  351.7 1.2 multiply_reduce_fusion
  352.8 77.5 %psum.37 = f32[128]{0:T(128)S(1)} all-reduce(f32[128]{0:T(128)S(1)} %get-tuple-element.6), channel_id=1, replica_groups=mesh['row'=16,'col'=16] {'row','col'}, use_global_device_ids=true, to_apply=%region_5.0 | all-reduce | flops 128 | bytes 1024 | tf_op jit(solution)/shard_map/psum | solution.py:38
  430.3 0.9 fusion.36
  431.3 15.8 %all_gather.7 = f32[512,128]{1,0:T(8,128)S(1)} all-gather(f32[32,128]{1,0:T(8,128)S(1)} %broadcast_divide_fusion), channel_id=1, replica_groups=mesh['row'=16,'col'=16] {'col'}, dimensions={0}, use_global_device_ids=true | all-gather | bytes 278528 | tf_op jit(solution)/shard_map/all_gather | solution.py:42
  447.1 0.3 all-reduce.9.cloned.1.call-start
  447.3 11.4 %fusion.11 = f32[512,128]{0,1:T(8,128)} fusion(f32[12,512,512]{2,1,0:T(8,128)} %param.6, f32[512,128]{1,0:T(8,128)S(1)} %all_gather.7, f32[12,128]{1,0:T(8,128)S(1)} %copy-done), kind=kOutput, calls=%fused_computation.9 | convolution fusion | flops 4832624640 | bytes 13113344 | tf_op jit(solution)/shard_map/kij,kir->jr/dot_general | solution.py:43
  458.8 234.0 %all-reduce.11.cloned.1.call-done = f32[128,128]{0,1:T(8,128)} async-done(((f32[128,128]{0,1:T(8,128)}), f32[128,128]{0,1:T(8,128)}) %all-reduce.11.cloned.1.call-update) | async-done | bytes 65552 | tf_op jit(solution)/shard_map/psum | solution.py:40
  692.8 0.9 mul.48
  693.7 0.1 copy.10
  693.8 11.7 %cholesky.55 = f32[128,128]{1,0:T(8,128)S(1)} custom-call(f32[128,128]{1,0:T(8,128)S(1)} %fusion.23), custom_call_target="Cholesky" | custom-call | tf_op jit(solution)/shard_map/jit(cholesky)/cholesky | solution.py:11
  705.5 0.6 compare_reduce_fusion
  706.2 0.7 fusion.19
  706.8 9.8 %custom-call.9 = f32[1,128,128]{1,2,0:T(8,128)S(1)} custom-call(f32[1,128,128]{2,1,0:T(8,128)S(1)} %fusion.19), custom_call_target="InvertDiagBlocksLowerTriangular" | custom-call | tf_op jit(solution)/shard_map/jit(_cho_solve)/triangular_solve | solution.py:12
  716.7 0.3 fusion.14
  716.9 0.2 fusion.20
  717.2 84.3 %all-reduce.9.cloned.1.call-done = f32[512,128]{0,1:T(8,128)} async-done(((f32[512,128]{0,1:T(8,128)}), f32[512,128]{0,1:T(8,128)}) %all-reduce.9.cloned.1.call-update) | async-done | bytes 262160 | tf_op jit(solution)/shard_map/psum | solution.py:44
  801.4 1.8 fusion.28
  (15 shorter events, 0.2 us)
Async XLA Ops:
  7.2 251.9 %all-reduce.7.cloned.1.call-start = ((), (), s32[]{:S(2)}) async-start(), calls=%async_computation.1 | async-start | bytes 131072 | tf_op jit(solution)/shard_map/psum | solution.py:31
  8.9 342.7 %all-reduce.5.cloned.1.call-start = ((), (), s32[]{:S(2)}) async-start(), calls=%async_computation | async-start | bytes 524288 | tf_op jit(solution)/shard_map/psum | solution.py:35
  31.2 227.8 %copy-start = (f32[12,128]{1,0:T(8,128)S(1)}, f32[12,128]{1,0:T(8,128)}, u32[]{:S(2)}) copy-start(f32[12,128]{1,0:T(8,128)} %param.8) | copy-start | bytes 18436
  49.6 643.2 %all-reduce.11.cloned.1.call-start = ((), (), s32[]{:S(2)}) async-start(), calls=%async_computation.3 | async-start | bytes 131072 | tf_op jit(solution)/shard_map/psum | solution.py:40
  352.8 105.9 %copy-start.1 = (f32[32,128]{1,0:T(8,128)}, f32[32,128]{1,0:T(8,128)S(1)}, u32[]{:S(2)}) copy-start(f32[32,128]{1,0:T(8,128)S(1)} %get-tuple-element.7) | copy-start | bytes 49156
  447.1 354.4 %all-reduce.9.cloned.1.call-start = ((), (), s32[]{:S(2)}) async-start(), calls=%async_computation.2 | async-start | bytes 524288 | tf_op jit(solution)/shard_map/psum | solution.py:44
Sparse Core Ops, SparseCore 0:
  13.5 245.5 all-reduce.6
  262.2 89.3 all-reduce.4
  447.2 245.5 all-reduce.10
  695.0 106.4 all-reduce.8
where the time goes:
time: 810 us
  waiting for transfers between devices  596 us (74%)
  blocking collectives  116 us (14%)
  other arithmetic  46.6 us (6%)
  matrix products  37.4 us (5%)
  between operations  13.9 us (2%)
    psum x1, waiting for transfers between devices, per_device(): gram_a = lax.psum(gram_of(factor_a), ('row', 'col'))  234 us
    psum x1, waiting for transfers between devices, per_device(): gram_b = lax.psum(gram_of(factor_b), ('row', 'col'))  209 us
    psum x1, waiting for transfers between devices, per_device(): whole_b = lax.psum(partial_b, 'row')  84.3 us
    psum x1, blocking collectives, per_device(): squares = lax.psum(jnp.sum(a_update * a_update, axis=0), ('row', 'col'))  77.5 us
    psum x1, waiting for transfers between devices, per_device(): whole_a = lax.psum(partial_a, 'col')  68 us
    another operation x6, other arithmetic, solve_system(): lower = jnp.linalg.cholesky(system)  24.8 us
    all_gather x1, blocking collectives, per_device(): lax.all_gather(factor_b, 'row', axis=0, tiled=True)[None, :, :]  22.3 us
    another operation x4, other arithmetic, solve_system(): jax.scipy.linalg.cho_solve((lower, True), jnp.eye(system.shape[0], dtype=...  20.9 us
  transfers between devices with their start and end apart: 4, of which 4 were waited for; matrix products, arithmetic and copies ran while one was open for 10% of the time, Pallas kernels for 0%

commit v1 on v0

--- a/solution.py
+++ b/solution.py
@@ -20,6 +20,11 @@
 
 
 def per_device(tensor, factor_b, factor_c):
+
+    def trace_the_runs(local_values, axis_id):
+        carry = jnp.sum(jax.lax.all_gather(local_values, axis_name=axis_id), axis=0)
+        return carry
+
     highest = lax.Precision.HIGHEST
     rows_block = tensor.shape[1]
     cols_block = tensor.shape[2]
@@ -37,7 +42,7 @@
     a_update = solve_system(summed_a, c_gram * gram_b)
     squares = lax.psum(jnp.sum(a_update * a_update, axis=0), ("row", "col"))
     factor_a = a_update / jnp.sqrt(squares + EPSILON)
-    gram_a = lax.psum(gram_of(factor_a), ("row", "col"))
+    gram_a = trace_the_runs(gram_of(factor_a), ("row", "col"))
     block = tensor
     khatri = factor_c[:, None, :] * lax.all_gather(factor_a, "col", axis=0, tiled=True)[None, :, :]
     partial_b = empty_b + jnp.einsum("kij,kir->jr", block, khatri, precision=highest)

time: 810 us -> 671 us (0.83)
  waiting for transfers between devices: 596 us -> 452 us
    psum x1 -> x0, waiting for transfers between devices: 234 us -> none  [per_device(): gram_a = lax.psum(gram_of(factor_a), ('row', 'col'))]
    all_gather x0 -> x1, waiting for transfers between devices: none -> 94.3 us  [trace_the_runs(): carry = jnp.sum(jax.lax.all_gather(local_values, axis_name=axis_id), axis=0)]
  transfers between devices with their start and end apart: 4 -> 4, of which waited for: 4 -> 4; matrix products, arithmetic and copies ran while one was open for 10% -> 12% of each run, Pallas kernels for 0% -> 0%
where the time goes in v1:
time: 671 us
  waiting for transfers between devices  452 us (67%)
  blocking collectives  116 us (17%)
  other arithmetic  52.3 us (8%)
  matrix products  36 us (5%)
  between operations  13.9 us (2%)
    psum x1, waiting for transfers between devices, per_device(): gram_b = lax.psum(gram_of(factor_b), ('row', 'col'))  211 us
    all_gather x1, waiting for transfers between devices, trace_the_runs(): carry = jnp.sum(jax.lax.all_gather(local_values, axis_name=axis_id), axis=0)  94.3 us
    psum x1, waiting for transfers between devices, per_device(): whole_b = lax.psum(partial_b, 'row')  78.9 us
    psum x1, blocking collectives, per_device(): squares = lax.psum(jnp.sum(a_update * a_update, axis=0), ('row', 'col'))  77.5 us
    psum x1, waiting for transfers between devices, per_device(): whole_a = lax.psum(partial_a, 'col')  68 us
    another operation x6, other arithmetic, solve_system(): lower = jnp.linalg.cholesky(system)  24.8 us
    all_gather x1, blocking collectives, per_device(): lax.all_gather(factor_b, 'row', axis=0, tiled=True)[None, :, :]  22.3 us
    another operation x4, other arithmetic, solve_system(): jax.scipy.linalg.cho_solve((lower, True), jnp.eye(system.shape[0], dtype=...  20.9 us
  transfers between devices with their start and end apart: 4, of which 4 were waited for; matrix products, arithmetic and copies ran while one was open for 12% of the time, Pallas kernels for 0%

profile of v1, /device:TPU:1, one launch (start us, length us, event | category | flops | bytes accessed | tf_op | source)
XLA Modules:
  0.0 671.0 jit_solution(2305239293389513318)
XLA Ops:
  7.2 1.7 fusion.35
  8.9 0.0 all-reduce.4.cloned.1.call-start
  9.0 22.3 %all_gather.12 = f32[512,128]{1,0:T(8,128)S(1)} all-gather(f32[32,128]{1,0:T(8,128)} %param.7), channel_id=1, replica_groups=mesh['row'=16,'col'=16] {'row'}, dimensions={0}, use_global_device_ids=true | all-gather | bytes 278528 | tf_op jit(solution)/shard_map/all_gather | solution.py:38
  31.3 16.8 %fusion.8 = f32[512,128]{0,1:T(8,128)} fusion(f32[12,512,512]{2,1,0:T(8,128)} %param.6, f32[512,128]{1,0:T(8,128)S(1)} %all_gather.12, f32[12,128]{1,0:T(8,128)} %param.8), kind=kOutput, calls=%fused_computation.8 | convolution fusion | flops 4832624640 | bytes 13113344 | tf_op jit(solution)/shard_map/kij,kjr->ir/dot_general | solution.py:39
  48.1 0.2 all-gather.3.cloned.1.call-start
  48.3 210.7 %all-reduce.6.cloned.1.call-done = f32[128,128]{0,1:T(8,128)} async-done(((f32[128,128]{0,1:T(8,128)}), f32[128,128]{0,1:T(8,128)}) %all-reduce.6.cloned.1.call-update) | async-done | bytes 65552 | tf_op jit(solution)/shard_map/psum | solution.py:36
  259.1 1.1 fusion.34
  260.2 0.1 copy.12
  260.3 11.7 %cholesky.44 = f32[128,128]{1,0:T(8,128)S(1)} custom-call(f32[128,128]{1,0:T(8,128)S(1)} %fusion.27), custom_call_target="Cholesky" | custom-call | tf_op jit(solution)/shard_map/jit(cholesky)/cholesky | solution.py:11
  272.1 0.6 compare_reduce_fusion.1
  272.7 0.7 fusion.18
  273.4 9.8 %custom-call.8 = f32[1,128,128]{1,2,0:T(8,128)S(1)} custom-call(f32[1,128,128]{2,1,0:T(8,128)S(1)} %fusion.18), custom_call_target="InvertDiagBlocksLowerTriangular" | custom-call | tf_op jit(solution)/shard_map/jit(_cho_solve)/triangular_solve | solution.py:12
  283.2 0.3 fusion.16
  283.5 0.2 fusion.24
  283.7 68.0 %all-reduce.4.cloned.1.call-done = f32[512,128]{0,1:T(8,128)} async-done(((f32[512,128]{0,1:T(8,128)}), f32[512,128]{0,1:T(8,128)}) %all-reduce.4.cloned.1.call-update) | async-done | bytes 262160 | tf_op jit(solution)/shard_map/psum | solution.py:40
  351.7 1.2 multiply_reduce_fusion
  352.9 77.5 %psum.30 = f32[128]{0:T(128)S(1)} all-reduce(f32[128]{0:T(128)S(1)} %get-tuple-element.6), channel_id=1, replica_groups=mesh['row'=16,'col'=16] {'row','col'}, use_global_device_ids=true, to_apply=%region_5.0 | all-reduce | flops 128 | bytes 1024 | tf_op jit(solution)/shard_map/psum | solution.py:43
  430.3 0.9 fusion.36
  431.3 16.5 %all_gather.13 = f32[512,128]{1,0:T(8,128)S(1)} all-gather(f32[32,128]{1,0:T(8,128)S(1)} %broadcast_divide_fusion), channel_id=1, replica_groups=mesh['row'=16,'col'=16] {'col'}, dimensions={0}, use_global_device_ids=true | all-gather | bytes 278528 | tf_op jit(solution)/shard_map/all_gather | solution.py:47
  447.8 11.4 %fusion.11 = f32[512,128]{0,1:T(8,128)} fusion(f32[12,512,512]{2,1,0:T(8,128)} %param.6, f32[512,128]{1,0:T(8,128)S(1)} %all_gather.13, f32[12,128]{1,0:T(8,128)S(1)} %copy-done), kind=kOutput, calls=%fused_computation.9 | convolution fusion | flops 4832624640 | bytes 13113344 | tf_op jit(solution)/shard_map/kij,kir->jr/dot_general | solution.py:48
  459.3 94.3 %all-gather.3.cloned.1.call-done = f32[32768,128]{1,0:T(8,128)} async-done(((f32[128,128]{1,0:T(8,128)}), f32[32768,128]{1,0:T(8,128)}) %all-gather.3.cloned.1.call-update) | async-done | bytes 16777232 | tf_op jit(solution)/shard_map/all_gather | solution.py:25
  553.6 6.6 reduce_sum.19
  560.2 0.1 copy.14
  560.3 0.1 copy.15
  560.4 11.7 %cholesky.55 = f32[128,128]{1,0:T(8,128)S(1)} custom-call(f32[128,128]{1,0:T(8,128)S(1)} %fusion.23), custom_call_target="Cholesky" | custom-call | tf_op jit(solution)/shard_map/jit(cholesky)/cholesky | solution.py:11
  572.1 0.6 compare_reduce_fusion
  572.8 0.7 fusion.19
  573.5 9.8 %custom-call.9 = f32[1,128,128]{1,2,0:T(8,128)S(1)} custom-call(f32[1,128,128]{2,1,0:T(8,128)S(1)} %fusion.19), custom_call_target="InvertDiagBlocksLowerTriangular" | custom-call | tf_op jit(solution)/shard_map/jit(_cho_solve)/triangular_solve | solution.py:12
  583.3 0.3 fusion.14
  583.6 0.2 fusion.20
  583.8 78.9 %all-reduce.8.cloned.1.call-done = f32[512,128]{0,1:T(8,128)} async-done(((f32[512,128]{0,1:T(8,128)}), f32[512,128]{0,1:T(8,128)}) %all-reduce.8.cloned.1.call-update) | async-done | bytes 262160 | tf_op jit(solution)/shard_map/psum | solution.py:49
  662.7 1.8 fusion.28
  (17 shorter events, 0.3 us)
Async XLA Ops:
  7.2 251.9 %copy-start = (f32[12,128]{1,0:T(8,128)S(1)}, f32[12,128]{1,0:T(8,128)}, u32[]{:S(2)}) copy-start(f32[12,128]{1,0:T(8,128)} %param.8) | copy-start | bytes 18436
  7.2 251.9 %all-reduce.6.cloned.1.call-start = ((), (), s32[]{:S(2)}) async-start(), calls=%async_computation.1 | async-start | bytes 131072 | tf_op jit(solution)/shard_map/psum | solution.py:36
  8.9 342.7 %all-reduce.4.cloned.1.call-start = ((), (), s32[]{:S(2)}) async-start(), calls=%async_computation | async-start | bytes 524288 | tf_op jit(solution)/shard_map/psum | solution.py:40
  48.1 505.5 %all-gather.3.cloned.1.call-start = ((), (), s32[]{:S(2)}) async-start(), calls=%async_computation.3 | async-start | bytes 16842752 | tf_op jit(solution)/shard_map/all_gather | solution.py:25
  352.8 207.3 %copy-start.1 = (f32[32,128]{1,0:T(8,128)}, f32[32,128]{1,0:T(8,128)S(1)}, u32[]{:S(2)}) copy-start(f32[32,128]{1,0:T(8,128)S(1)} %get-tuple-element.7) | copy-start | bytes 49156
  431.3 231.4 %all-reduce.8.cloned.1.call-start = ((), (), s32[]{:S(2)}) async-start(), calls=%async_computation.2 | async-start | bytes 524288 | tf_op jit(solution)/shard_map/psum | solution.py:49
Sparse Core Ops, SparseCore 0:
  13.5 245.5 all-reduce.5
  262.2 89.3 all-reduce.3
  431.4 122.1 all-gather.2
  555.7 106.8 all-reduce.7
